TPU v7x, 32 devices: a whole 2x2x4 slice. The times are simulated.
32 devices in a mesh: heads: 4 (over y, x), seq: 8 (over z, core).
Axes of the slice: x: 2, y: 2, z: 4, core: 2. Of those that a mesh axis runs over, the one named last changes fastest.
Arguments:
- local_qkv: bfloat16 [3, 4096, 2048], P(None, 'seq', 'heads'), may hold values from -8 to 8
- routed_qkv: bfloat16 [3, 4096, 2048], P(None, 'seq', 'heads'), may hold values from -8 to 8
- clusters: int32 [16, 4096], P('heads', 'seq'), may hold values from 0 to 127, as said below
- wo_local: bfloat16 [2048, 4096], P('heads'), may hold values from -0.5 to 0.5
- wo_routed: bfloat16 [2048, 4096], P('heads'), may hold values from -0.5 to 0.5
Outputs:
- layer_out: bfloat16 [4096, 4096], P('seq', 'heads')
Inputs may be any that keep to these rules, and one draw needn't show every extreme that they name: `clusters`: in every routed head, no cluster holds more than 8 of the 512 tokens of one aligned block of tokens; in every head and block some cluster holds exactly 8 of them.
All inputs are finite; a program needn't handle non-finite values.
Results may differ from a plain program's by a relative error of at most 0.009.
Values may be sent and summed in bfloat16 or wider, within the bound.
A program may use at most 128 MiB of HBM per device.

v0:
```python
import jax
import jax.numpy as jnp
from jax import lax
from jax.sharding import PartitionSpec as P

DH = 128
WINDOW = 512
NCLUST = 128


masked_fill = -1e30


def passed_along(block, axis, distance):
    devices = range(lax.axis_size(axis))
    route = [(i - distance, i) for i in devices if i - distance in devices]
    return lax.ppermute(block, axis, route)


def soft_weights(scores, allowed):
    scores = jnp.where(allowed, scores, masked_fill)
    top_score = jnp.max(scores, axis=-1, keepdims=True)
    raised = jnp.exp(scores - top_score)
    return (raised / jnp.sum(raised, axis=-1, keepdims=True)).astype(jnp.bfloat16)


def window_part(local_qkv):
    tok_count = local_qkv.shape[1]
    width = local_qkv.shape[2]
    head_count = width // DH
    seq_index = lax.axis_index("seq")
    earlier = passed_along(local_qkv[1:], "seq", 1)
    joined = jnp.concatenate([earlier, local_qkv[1:]], axis=1)
    queries = local_qkv[0].reshape(tok_count, head_count, DH)
    keys_all = joined[0].reshape(2 * tok_count, head_count, DH)
    values_all = joined[1].reshape(2 * tok_count, head_count, DH)

    def one_block(index):
        start = index * WINDOW
        scores = jnp.einsum(
            "qhd,khd->hqk", queries, keys_all, preferred_element_type=jnp.float32
        ) * DH ** (-0.5)
        query_at = start + jnp.arange(WINDOW, dtype=jnp.int32)
        key_index = tok_count + start - WINDOW + jnp.arange(2 * WINDOW, dtype=jnp.int32)
        offset = (key_index - tok_count)[None, :] - query_at[:, None]
        present = (seq_index > 0) | (key_index >= tok_count)
        allowed = (offset <= 0) & (offset > -WINDOW) & present[None, :]
        weights = soft_weights(scores, allowed[None])
        result = jnp.einsum("hqk,khd->qhd", weights, values_all, preferred_element_type=jnp.float32)
        return result.astype(jnp.bfloat16).reshape(WINDOW, width)

    blocks = lax.map(one_block, jnp.arange(tok_count // WINDOW, dtype=jnp.int32))
    return blocks.reshape(tok_count, width)


def routed_part(routed_qkv, clusters):
    tok_count = routed_qkv.shape[1]
    head_count = clusters.shape[0]
    seq_count = lax.axis_size("seq")
    seq_index = lax.axis_index("seq")
    most_rows = 2 * tok_count // NCLUST
    slot_total = NCLUST * most_rows
    per_owner = slot_total // seq_count
    onehot = (clusters[:, :, None] == jnp.arange(NCLUST, dtype=jnp.int32)[None, None, :]).astype(
        jnp.int32
    )
    before = jnp.cumsum(onehot, axis=1) - onehot
    rank_index = jnp.sum(before * onehot, axis=-1)
    slot_index = clusters * most_rows + rank_index
    head_index = jnp.broadcast_to(
        jnp.arange(head_count, dtype=jnp.int32)[:, None], (head_count, tok_count)
    )
    token_ids = jnp.broadcast_to(
        jnp.arange(tok_count, dtype=jnp.int32)[None, :], (head_count, tok_count)
    )
    token_at = (
        jnp.full((head_count, slot_total), -1, jnp.int32).at[head_index, slot_index].set(token_ids)
    )
    row_data = (
        routed_qkv.reshape(3, tok_count, head_count, DH)
        .transpose(2, 1, 0, 3)
        .reshape(head_count, tok_count, 3 * DH)
    )
    picked = jnp.take_along_axis(row_data, jnp.maximum(token_at, 0)[:, :, None], axis=1)
    picked = jnp.where(token_at[:, :, None] >= 0, picked, jnp.zeros_like(picked))
    positions = jnp.where(token_at >= 0, seq_index * tok_count + token_at, -1)
    send_rows = picked.reshape(head_count, seq_count, per_owner, 3 * DH)
    send_places = positions.reshape(head_count, seq_count, per_owner)
    rows_in = lax.all_to_all(send_rows, "seq", split_axis=1, concat_axis=1, tiled=True)
    places_in = lax.all_to_all(send_places, "seq", split_axis=1, concat_axis=1, tiled=True)
    item_count = rows_in.shape[0]
    owned = per_owner // most_rows
    members = seq_count * most_rows
    grouped = rows_in.reshape(item_count, seq_count, owned, most_rows, 3 * DH).transpose(
        0, 2, 1, 3, 4
    )
    grouped = grouped.reshape(item_count, owned, members, 3 * DH)
    places = places_in.reshape(item_count, seq_count, owned, most_rows).transpose(0, 2, 1, 3)
    places = places.reshape(item_count, owned, members)
    scores = jnp.einsum(
        "ncqd,nckd->ncqk",
        grouped[..., :DH],
        grouped[..., DH : 2 * DH],
        preferred_element_type=jnp.float32,
    ) * DH ** (-0.5)
    allowed = (places[:, :, None, :] >= 0) & (places[:, :, None, :] <= places[:, :, :, None])
    weights = soft_weights(scores, allowed)
    result = jnp.einsum(
        "ncqk,nckd->ncqd", weights, grouped[..., 2 * DH :], preferred_element_type=jnp.float32
    )
    result = (
        result.astype(jnp.bfloat16)
        .reshape(item_count, owned, seq_count, most_rows, DH)
        .transpose(0, 2, 1, 3, 4)
    )
    result = result.reshape(item_count, seq_count, per_owner, DH)
    returned = lax.all_to_all(result, "seq", split_axis=1, concat_axis=1, tiled=True)
    returned = returned.reshape(head_count, slot_total, DH)
    mine = jnp.take_along_axis(returned, slot_index[:, :, None], axis=1)
    return mine.transpose(1, 0, 2).reshape(tok_count, head_count * DH)


def body(local_qkv, routed_qkv, clusters, wo_local, wo_routed):
    local_out = window_part(local_qkv)
    routed_out = routed_part(routed_qkv, clusters)
    group_sum = jnp.dot(local_out, wo_local, preferred_element_type=jnp.float32)
    group_sum = group_sum + jnp.dot(routed_out, wo_routed, preferred_element_type=jnp.float32)
    summed = lax.psum_scatter(
        group_sum.astype(jnp.bfloat16), "heads", scatter_dimension=1, tiled=True
    )
    return summed


def solution(mesh):
    return jax.shard_map(
        body,
        mesh=mesh,
        in_specs=(
            P(None, "seq", "heads"),
            P(None, "seq", "heads"),
            P("heads", "seq"),
            P("heads", None),
            P("heads", None),
        ),
        out_specs=P("seq", "heads"),
        check_vma=False,
    )
```

profile of v0, /device:TPU:16, one launch (start us, length us, event | category | flops | bytes accessed | tf_op | source)
XLA Modules:
  0.0 280.9 jit_solution(4169439975950401828)
XLA Ops:
  6.5 0.7 eq.26
  7.4 0.9 fusion.21
  9.0 0.6 fusion.19
  9.9 8.1 %scatter_custom_fusion = s32[4096]{0:T(1024)S(1)} fusion(s32[2048]{0:T(1024)S(1)} %bitcast.109, s32[2048]{0:T(1024)S(1)} %bitcast.108, s32[]{:T(128)} %constant.87.clone.1), kind=kCustom, calls=%fused_computation.62 | custom fusion | bytes 16388
  18.0 0.6 copy.75
  18.6 5.2 %all-to-all-start = ((s32[4,8,128]{2,0,1:T(4,128)}), s32[4,8,128]{2,0,1:T(4,128)S(1)}, u32[]{:S(2)}, u32[]{:S(2)}) async-start(s32[4,8,128]{2,0,1:T(4,128)} %copy.75), calls=%async_computation | async-start | bytes 32768 | tf_op jit(solution)/shard_map/all_to_all | solution.py:90
  23.9 0.7 copy.83
  24.7 0.9 copy.85
  25.6 44.7 %gather_fusion = bf16[4096,384]{1,0:T(8,128)(2,1)} fusion(bf16[4,512,384]{2,1,0:T(8,128)(2,1)S(1)} %copy.85, s32[4096]{0:T(1024)S(1)} %bitcast.93), kind=kCustom, calls=%fused_computation | custom fusion | bytes 6324224 | tf_op jit(solution)/shard_map/jit(take_along_axis)/gather | solution.py:84
  70.4 4.8 %fusion.7 = bf16[4,8,128,384]{3,2,0,1:T(8,128)(2,1)} fusion(bf16[4,8,128,384]{3,2,1,0:T(8,128)(2,1)} %bitcast.96, pred[4,8,128]{2,0,1:T(4,128)(4,1)S(1)} %copy.82, pred[4,8,128]{2,0,1:T(4,128)(4,1)S(1)} %copy.81), kind=kLoop, calls=%fused_computation.16 | loop fusion | flops 3145728 | bytes 6299648 | tf_op jit(solution)/shard_map/jit(_where)/select_n | solution.py:85
  75.2 5.1 %all-to-all-start.1 = ((bf16[4,8,128,384]{3,2,0,1:T(8,128)(2,1)}), bf16[4,8,128,384]{3,2,0,1:T(8,128)(2,1)S(1)}, u32[]{:S(2)}, u32[]{:S(2)}) async-start(bf16[4,8,128,384]{3,2,0,1:T(8,128)(2,1)} %fusion.7), calls=%async_computation.1 | async-start | bytes 6291456 | tf_op jit(solution)/shard_map/all_to_all | solution.py:89
  80.3 2.3 slice.28
  82.5 2.3 copy.99
  84.8 2.0 collective-permute-start
  86.9 1.9 slice.31
  88.7 2.1 copy.100
  90.9 1.6 fusion.11
  93.0 67.6 %collective-permute-done = bf16[2,512,512]{1,2,0:T(8,128)(2,1)} collective-permute-done((bf16[2,512,512]{1,2,0:T(8,128)(2,1)}, bf16[2,512,512]{1,2,0:T(8,128)(2,1)}, u32[]{:S(2)}, u32[]{:S(2)}) %collective-permute-start) | collective-permute-done | bytes 1048608 | tf_op jit(solution)/shard_map/ppermute | solution.py:17
  160.6 3.2 %pad_maximum_fusion = (bf16[1,1024,512]{1,2,0:T(8,128)(2,1)}, bf16[1,1024,512]{1,2,0:T(8,128)(2,1)}) fusion(bf16[2,512,512]{1,2,0:T(8,128)(2,1)} %copy.99, bf16[2,512,512]{1,2,0:T(8,128)(2,1)} %collective-permute-done), kind=kLoop, calls=%fused_computation.34 | loop fusion | flops 4194304 | bytes 4194304 | tf_op jit(solution)/shard_map/concatenate | solution.py:33
  163.8 0.6 copy_bitcast_fusion
  164.4 3.2 %multiply_select_fusion = f32[4,16,64,64]{2,3,1,0:T(8,128)S(1)} fusion(bf16[4,16,64,384]{3,2,1,0:T(8,128)(2,1)S(1)} %copy_bitcast_fusion, s32[4,16,64]{2,1,0:T(8,128)S(1)} %copy.79, pred[4,16,64]{2,1,0:T(8,128)(4,1)S(1)} %copy.78), kind=kOutput, calls=%fused_computation.21 | convolution fusion | flops 68157440 | bytes 3219456 | tf_op jit(solution)/shard_map/ncqd,nckd->ncqk/dot_general | solution.py:100
  167.6 0.5 fusion.35
  168.1 2.0 fusion.12
  170.4 1.0 copy.91
  171.4 4.2 %all-to-all-start.2 = ((bf16[4,8,128,128]{3,2,0,1:T(8,128)(2,1)}), bf16[4,8,128,128]{3,2,0,1:T(8,128)(2,1)S(1)}, u32[]{:S(2)}, u32[]{:S(2)}) async-start(bf16[4,8,128,128]{3,2,0,1:T(8,128)(2,1)} %copy.91), calls=%async_computation.2 | async-start | bytes 2097152 | tf_op jit(solution)/shard_map/all_to_all | solution.py:117
  175.6 7.9 %fusion.34 = (f32[4,512]{1,0:T(4,128)S(1)}, f32[4,512,1024]{1,2,0:T(8,128)}) fusion(pred[512,1024]{0,1:T(8,128)(4,1)} %fusion.11, bf16[1024,4,128]{0,2,1:T(8,128)(2,1)S(1)} %bitcast.105, bf16[512,4,128]{0,2,1:T(8,128)(2,1)} %bitcast.107), kind=kOutput, calls=%fused_computation.74 | convolution fusion | flops 545260544 | bytes 10493952 | tf_op jit(solution)/shard_map/while/body/eval_jaxpr/sub | solution.py:23
  183.5 4.3 %fusion.13 = bf16[4,128,512]{2,1,0:T(8,128)(2,1)S(1)} fusion(bf16[1024,4,128]{0,2,1:T(8,128)(2,1)S(1)} %bitcast.104, f32[4,512,1024]{1,2,0:T(8,128)} %get-tuple-element.30, f32[4,512]{1,0:T(4,128)S(1)} %get-tuple-element.29), kind=kOutput, calls=%fused_computation.29 | convolution fusion | flops 541327360 | bytes 9969664 | tf_op jit(solution)/shard_map/while/body/eval_jaxpr/hqk,khd->qhd/dot_general | solution.py:49
  188.1 5.6 %fusion.36 = f32[512,4096]{1,0:T(8,128)} fusion(bf16[512,512]{0,1:T(8,128)(2,1)S(1)} %bitcast.106, bf16[512,4096]{1,0:T(8,128)(2,1)S(1)} %copy-done), kind=kOutput, calls=%fused_computation.76 | convolution fusion | flops 2147483648 | bytes 13107200 | tf_op jit(solution)/shard_map/dot_general | solution.py:126
  193.7 5.2 %all-to-all-done.2 = bf16[4,8,128,128]{3,2,0,1:T(8,128)(2,1)S(1)} async-done(((bf16[4,8,128,128]{3,2,0,1:T(8,128)(2,1)}), bf16[4,8,128,128]{3,2,0,1:T(8,128)(2,1)S(1)}, u32[]{:S(2)}, u32[]{:S(2)}) %all-to-all-start.2) | async-done | bytes 1048608 | tf_op jit(solution)/shard_map/all_to_all | solution.py:117
  199.1 11.1 %gather_fusion.1 = bf16[2048,128]{1,0:T(8,128)(2,1)S(1)} fusion(bf16[4,1024,128]{2,1,0:T(8,128)(2,1)S(1)} %bitcast.95, s32[2048]{0:T(1024)S(1)} %bitcast.94), kind=kCustom, calls=%fused_computation.1 | custom fusion | bytes 1064960 | tf_op jit(solution)/shard_map/jit(take_along_axis)/gather | solution.py:119
  210.5 9.0 %add_convert_fusion = bf16[512,4096]{1,0:T(8,128)(2,1)} fusion(f32[512,4096]{1,0:T(8,128)} %fusion.36, bf16[512,512]{0,1:T(8,128)(2,1)S(1)} %bitcast.100, bf16[512,4096]{1,0:T(8,128)(2,1)} %param.9), kind=kOutput, calls=%fused_computation.6 | convolution fusion | flops 2151677952 | bytes 17301504 | tf_op jit(solution)/shard_map/dot_general | solution.py:127
  219.5 54.5 %reduce-scatter.2.cloned.1.call-done = bf16[512,1024]{1,0:T(8,128)(2,1)} async-done(((bf16[512,4096]{1,0:T(8,128)(2,1)}), bf16[512,1024]{1,0:T(8,128)(2,1)}) %reduce-scatter.2.cloned.1.call-update) | async-done | bytes 1048592 | tf_op jit(solution)/shard_map/reduce_scatter | solution.py:128
  (57 shorter events, 2.6 us)
Async XLA Ops:
  8.3 0.7 copy-start.5
  8.5 1.2 copy-start.7
  8.5 1.2 copy-start.6
  8.6 15.3 %copy-start.2 = (bf16[3,512,512]{2,1,0:T(8,128)(2,1)S(1)}, bf16[3,512,512]{2,1,0:T(8,128)(2,1)}, u32[]{:S(2)}) copy-start(bf16[3,512,512]{2,1,0:T(8,128)(2,1)} %param.6) | copy-start | bytes 4718596
  18.6 56.6 %all-to-all-start = ((s32[4,8,128]{2,0,1:T(4,128)}), s32[4,8,128]{2,0,1:T(4,128)S(1)}, u32[]{:S(2)}, u32[]{:S(2)}) async-start(s32[4,8,128]{2,0,1:T(4,128)} %copy.75), calls=%async_computation | async-start | bytes 32768 | tf_op jit(solution)/shard_map/all_to_all | solution.py:90
  75.2 88.6 %all-to-all-start.1 = ((bf16[4,8,128,384]{3,2,0,1:T(8,128)(2,1)}), bf16[4,8,128,384]{3,2,0,1:T(8,128)(2,1)S(1)}, u32[]{:S(2)}, u32[]{:S(2)}) async-start(bf16[4,8,128,384]{3,2,0,1:T(8,128)(2,1)} %fusion.7), calls=%async_computation.1 | async-start | bytes 6291456 | tf_op jit(solution)/shard_map/all_to_all | solution.py:89
  84.8 75.8 %collective-permute-start = (bf16[2,512,512]{1,2,0:T(8,128)(2,1)}, bf16[2,512,512]{1,2,0:T(8,128)(2,1)}, u32[]{:S(2)}, u32[]{:S(2)}) collective-permute-start(bf16[2,512,512]{1,2,0:T(8,128)(2,1)} %copy.99), channel_id=1, source_target_pairs={{0,1},{1,2},{2,3},{3,4},{4,5},{5,6},{6,7},{8,9},{9,10},{10,11},{11... | collective-permute-start | bytes 3145736 | tf_op jit(solution)/shard_map/ppermute | solution.py:17
  164.4 3.2 %copy-start.1 = (bf16[4,16,64,384]{3,2,1,0:T(8,128)(2,1)}, bf16[4,16,64,384]{3,2,1,0:T(8,128)(2,1)S(1)}, u32[]{:S(2)}) copy-start(bf16[4,16,64,384]{3,2,1,0:T(8,128)(2,1)S(1)} %copy_bitcast_fusion) | copy-start | bytes 9437188
  170.4 5.3 %copy-start.4 = (bf16[1,1024,512]{1,2,0:T(8,128)(2,1)S(1)}, bf16[1,1024,512]{1,2,0:T(8,128)(2,1)}, u32[]{:S(2)}) copy-start(bf16[1,1024,512]{1,2,0:T(8,128)(2,1)} %get-tuple-element.15) | copy-start | bytes 3145732
  171.4 27.5 %all-to-all-start.2 = ((bf16[4,8,128,128]{3,2,0,1:T(8,128)(2,1)}), bf16[4,8,128,128]{3,2,0,1:T(8,128)(2,1)S(1)}, u32[]{:S(2)}, u32[]{:S(2)}) async-start(bf16[4,8,128,128]{3,2,0,1:T(8,128)(2,1)} %copy.91), calls=%async_computation.2 | async-start | bytes 2097152 | tf_op jit(solution)/shard_map/all_to_all | solution.py:117
  175.6 98.4 %reduce-scatter.2.cloned.1.call-start = ((), (), s32[]{:S(2)}) async-start(), calls=%async_computation.4 | async-start | bytes 5242880 | tf_op jit(solution)/shard_map/reduce_scatter | solution.py:128
  175.6 7.9 %copy-start.3 = (bf16[1,1024,512]{1,2,0:T(8,128)(2,1)S(1)}, bf16[1,1024,512]{1,2,0:T(8,128)(2,1)}, u32[]{:S(2)}) copy-start(bf16[1,1024,512]{1,2,0:T(8,128)(2,1)} %get-tuple-element.16) | copy-start | bytes 3145732
  183.5 4.6 %copy-start = (bf16[512,4096]{1,0:T(8,128)(2,1)S(1)}, bf16[512,4096]{1,0:T(8,128)(2,1)}, u32[]{:S(2)}) copy-start(bf16[512,4096]{1,0:T(8,128)(2,1)} %param.8) | copy-start | bytes 12582916
Sparse Core Ops, SparseCore 0:
  219.7 54.3 reduce-scatter.1
where the time goes:
time: 283 us; the launch traced here: 281 us
  waiting for transfers between devices  127 us (45%)
  local copies, waits for them, and re-layouts  79 us (28%)
  matrix products  32 us (11%)
  starting transfers between devices  16.6 us (6%)
  between operations  13.8 us (5%)
  other arithmetic  12.2 us (4%)
    ppermute x1, waiting for transfers between devices, passed_along(): return lax.ppermute(block, axis, route)  67.6 us
    reduce_scatter x1, waiting for transfers between devices, body(): lax.psum_scatter(group_sum.astype(jnp.bfloat16), 'heads', scatter_dimensi...  54.5 us
    gather x2, local copies, waits for them, and re-layouts, routed_part(): jnp.take_along_axis(row_data, jnp.maximum(token_at, 0)[:, :, None], axis=1)  44.8 us
    unnamed x25, local copies, waits for them, and re-layouts  13.7 us
    gather x2, local copies, waits for them, and re-layouts, routed_part(): mine = jnp.take_along_axis(returned, slot_index[:, :, None], axis=1)  11.3 us
    dot_general x1, matrix products, body(): jnp.dot(routed_out, wo_routed, preferred_element_type=jnp.float32)  9.04 us
    sub x1, matrix products, soft_weights(): raised = jnp.exp(scores - top_score)  7.89 us
  transfers between devices with their start and end apart: 5, of which 3 were waited for; matrix products, arithmetic and copies ran while one was open for 30% of the time, Pallas kernels for 0%

commit v1 on v0

v1 whole, which is shorter than its diff:
```python
import functools
import math

import jax
import jax.numpy as jnp
from jax import lax
from jax.experimental import pallas as pl
from jax.experimental.pallas import tpu as pltpu
from jax.sharding import PartitionSpec as P

DH = 128
WINDOW = 512
MASKED = -1e30
SCALE2 = math.log2(math.e) / math.sqrt(DH)
VMEM_LIMIT = 56 << 20

NT = (((1,), (1,)), ((), ()))
MESH = pl.DeviceIdType.MESH


def vmem():
    return pl.BlockSpec(memory_space=pltpu.VMEM)


def dot_nt(a, b):
    return lax.dot_general(a, b, NT, preferred_element_type=jnp.float32)


def dot(a, b):
    return jnp.dot(a, b, preferred_element_type=jnp.float32)


def window_kernel(first_ref, own_ref, prev_ref, out_ref):
    tok_count, width = out_ref.shape
    rows = min(256, tok_count)
    span = rows + WINDOW
    is_first = first_ref[0] == 0
    for i in range(tok_count // rows):
        r = lax.broadcasted_iota(jnp.int32, (rows, span), 0)
        c = lax.broadcasted_iota(jnp.int32, (rows, span), 1)
        from_prev = WINDOW - i * rows
        lowest = jnp.where(is_first, from_prev, 0)
        allowed = (c > r) & (c <= r + WINDOW) & (c >= lowest)
        for h in range(width // DH):
            cols = slice(h * DH, (h + 1) * DH)
            q = own_ref[0, i * rows:(i + 1) * rows, cols]
            k = jnp.concatenate(
                [prev_ref[0, i * rows:, cols], own_ref[1, :(i + 1) * rows, cols]], axis=0)
            v = jnp.concatenate(
                [prev_ref[1, i * rows:, cols], own_ref[2, :(i + 1) * rows, cols]], axis=0)
            s = jnp.where(allowed, dot_nt(q, k), MASKED)
            top = jnp.max(s, axis=-1, keepdims=True)
            p = jnp.exp2((s - top) * SCALE2)
            total = jnp.sum(p, axis=-1, keepdims=True)
            o = dot(p.astype(jnp.bfloat16), v) / total
            out_ref[i * rows:(i + 1) * rows, cols] = o.astype(jnp.bfloat16)


def window_part(local_qkv):
    tok_count = local_qkv.shape[1]
    width = local_qkv.shape[2]
    n = lax.axis_size("seq")
    prev = lax.ppermute(local_qkv[1:], "seq", [(i, i + 1) for i in range(n - 1)])
    where_at = lax.axis_index("seq").astype(jnp.int32).reshape(1)
    return pl.pallas_call(
        window_kernel,
        out_shape=jax.ShapeDtypeStruct((tok_count, width), jnp.bfloat16),
        in_specs=[pl.BlockSpec(memory_space=pltpu.SMEM), vmem(), vmem()],
        out_specs=vmem(),
        cost_estimate=pl.CostEstimate(
            flops=4 * tok_count * 768 * width, bytes_accessed=6 << 20, transcendentals=2 << 20),
        compiler_params=pltpu.CompilerParams(vmem_limit_bytes=VMEM_LIMIT),
    )(where_at, local_qkv, prev)


def cluster_kernel(pair, r_ref, kv_ref, cq_ref, ck_ref, qpos_ref, kpos_ref, out_ref):
    n, rows, _ = out_ref.shape

    def keys(j, which):
        if pair:
            return jnp.concatenate([r_ref[j, 1 + which], kv_ref[j, which]], axis=0)
        return jnp.concatenate([kv_ref[p, j, which] for p in range(kv_ref.shape[0])], axis=0)

    def one_block(b, _):
        q = r_ref[b, 0]
        cq = cq_ref[b]

        def scores(j):
            return dot_nt(q, keys(j, 0)), cq == ck_ref[j]

        s, same = scores(b)
        s = jnp.where(same & (kpos_ref[...] <= qpos_ref[...]), s, MASKED)
        top = jnp.max(s, axis=-1, keepdims=True)
        p = jnp.exp2((s - top) * SCALE2)
        total = jnp.sum(p, axis=-1, keepdims=True)
        acc = dot(p.astype(jnp.bfloat16), keys(b, 1))

        def one_chunk(j, carry):
            top, total, acc = carry
            s, same = scores(j)
            s = jnp.where(same, s, MASKED)
            new_top = jnp.maximum(top, jnp.max(s, axis=-1, keepdims=True))
            fade = jnp.exp2((top - new_top) * SCALE2)
            p = jnp.exp2((s - new_top) * SCALE2)
            total = fade * total + jnp.sum(p, axis=-1, keepdims=True)
            acc = fade * acc + dot(p.astype(jnp.bfloat16), keys(j, 1))
            return new_top, total, acc

        top, total, acc = lax.fori_loop(0, b, one_chunk, (top, total, acc))
        out_ref[b] = (acc / total).astype(jnp.bfloat16)
        return 0

    lax.fori_loop(0, n, one_block, 0)


def routed_part(routed_qkv, clusters):
    tok_count = routed_qkv.shape[1]
    head_count = clusters.shape[0]
    n = lax.axis_size("seq")
    me = lax.axis_index("seq")
    group = n // head_count
    rows = tok_count // group
    part = me % group
    table = lax.all_gather(clusters, "seq")
    send = routed_qkv.reshape(3, group, rows, head_count, DH).transpose(3, 1, 0, 2, 4)
    send = send.reshape(n, 3, rows, DH)
    got = lax.all_to_all(send, "seq", split_axis=0, concat_axis=0, tiled=True)
    mine = lax.dynamic_index_in_dim(table, me // group, 1, keepdims=False)
    by_part = mine.reshape(n, group, rows)
    cq = lax.dynamic_index_in_dim(by_part, part, 1, keepdims=False)[:, :, None]
    at = jnp.arange(tok_count, dtype=jnp.int32).reshape(group, rows)
    qpos = lax.dynamic_index_in_dim(at, part, 0, keepdims=False)[:, None]
    pair = group == 2
    if pair:
        other = lax.ppermute(got[:, 1:], "seq", [(i, i + 1 - 2 * (i % 2)) for i in range(n)])
        ck = jnp.where(part == 0, by_part, by_part[:, ::-1])
        kpos = jnp.where(part == 0, at, at[::-1])
    else:
        groups = [[h * group + p for p in range(group)] for h in range(head_count)]
        other = lax.all_gather(got[:, 1:], "seq", axis_index_groups=groups)
        ck, kpos = by_part, at
    out = pl.pallas_call(
        functools.partial(cluster_kernel, pair),
        out_shape=jax.ShapeDtypeStruct((n, rows, DH), jnp.bfloat16),
        in_specs=[vmem()] * 6,
        out_specs=vmem(),
        compiler_params=pltpu.CompilerParams(vmem_limit_bytes=VMEM_LIMIT),
    )(got, other, cq, ck.reshape(n, 1, tok_count), qpos, kpos.reshape(1, tok_count))
    back = lax.all_to_all(out, "seq", split_axis=0, concat_axis=0, tiled=True)
    return back.reshape(head_count, tok_count, DH)


def project_kernel(n, local_ref, routed_ref, wl_ref, wr_ref, out_ref,
                   x, send, recv, send_sem, recv_sem):
    me = lax.axis_index("heads")
    tok_count, cols = out_ref.shape
    barrier = pltpu.get_barrier_semaphore()
    for k in range(1, n):
        pl.semaphore_signal(barrier, inc=1, device_id={"heads": lax.rem(me + k, n)},
                            device_id_type=MESH)
    for h in range(routed_ref.shape[0]):
        x[:, h * DH:(h + 1) * DH] = routed_ref[h]
    tile = min(512, cols)

    def product(owner, c):
        at = pl.ds(pl.multiple_of(owner * cols + c * tile, tile), tile)
        return dot(local_ref[...], wl_ref[:, at]) + dot(x[...], wr_ref[:, at])

    copies = []
    for k in range(1, n):
        owner = lax.rem(me + k, n)
        for c in range(cols // tile):
            send[k - 1, c] = product(owner, c).astype(jnp.bfloat16)
            if k == 1 and c == 0:
                pl.semaphore_wait(barrier, n - 1)
            copy = pltpu.make_async_remote_copy(
                src_ref=send.at[k - 1, c], dst_ref=recv.at[k - 1, c],
                send_sem=send_sem.at[k - 1, c], recv_sem=recv_sem.at[k - 1, c],
                device_id={"heads": owner}, device_id_type=MESH)
            copy.start()
            copies.append(copy)
    for c in range(cols // tile):
        total = product(me, c).astype(jnp.bfloat16).astype(jnp.float32)
        for k in range(1, n):
            copies[(k - 1) * (cols // tile) + c].wait_recv()
            total = total + recv[k - 1, c].astype(jnp.float32)
        out_ref[:, c * tile:(c + 1) * tile] = total.astype(jnp.bfloat16)
    for copy in copies:
        copy.wait_send()


def project(local_out, routed_out, wo_local, wo_routed):
    n = lax.axis_size("heads")
    tok_count = local_out.shape[0]
    cols = wo_local.shape[1] // n
    tile = min(512, cols)
    slots = (n - 1, cols // tile, tok_count, tile)
    return pl.pallas_call(
        functools.partial(project_kernel, n),
        out_shape=jax.ShapeDtypeStruct((tok_count, cols), jnp.bfloat16),
        in_specs=[vmem()] * 4,
        out_specs=vmem(),
        scratch_shapes=[
            pltpu.VMEM((tok_count, wo_routed.shape[0]), jnp.bfloat16),
            pltpu.VMEM(slots, jnp.bfloat16),
            pltpu.VMEM(slots, jnp.bfloat16),
            pltpu.SemaphoreType.DMA(slots[:2]),
            pltpu.SemaphoreType.DMA(slots[:2]),
        ],
        compiler_params=pltpu.CompilerParams(
            vmem_limit_bytes=VMEM_LIMIT, collective_id=0, has_side_effects=True),
    )(local_out, routed_out, wo_local, wo_routed)


def body(local_qkv, routed_qkv, clusters, wo_local, wo_routed):
    routed_out = routed_part(routed_qkv, clusters)
    local_out = window_part(local_qkv)
    return project(local_out, routed_out, wo_local, wo_routed)


def solution(mesh):
    return jax.shard_map(
        body,
        mesh=mesh,
        in_specs=(
            P(None, "seq", "heads"),
            P(None, "seq", "heads"),
            P("heads", "seq"),
            P("heads", None),
            P("heads", None),
        ),
        out_specs=P("seq", "heads"),
        check_vma=False,
    )
```

time: 283 us -> 171 us (0.60)
  the two profiles are of different devices: /device:TPU:16 before, /device:TPU:0 now
where the time goes in v1:
time: 171 us
  Pallas kernels  80.8 us (47%)
  blocking collectives  62.6 us (37%)
  local copies, waits for them, and re-layouts  11.3 us (7%)
  waiting for transfers between devices  9.48 us (6%)
  starting transfers between devices  6.53 us (4%)
    pallas_call x1, Pallas kernels, project(): pl.pallas_call(functools.partial(project_kernel, n), out_shape=jax.ShapeD...  53.7 us
    all_to_all x1, blocking collectives, routed_part(): got = lax.all_to_all(send, 'seq', split_axis=0, concat_axis=0, tiled=True)  44 us
    pallas_call x1, Pallas kernels, routed_part(): pl.pallas_call(functools.partial(cluster_kernel, pair), out_shape=jax.Sha...  21.2 us
    all_gather x1, blocking collectives, routed_part(): table = lax.all_gather(clusters, 'seq')  18.6 us
    all_to_all x1, waiting for transfers between devices, routed_part(): back = lax.all_to_all(out, 'seq', split_axis=0, concat_axis=0, tiled=True)  9.47 us
    pallas_call x1, Pallas kernels, window_part(): pl.pallas_call(window_kernel, out_shape=jax.ShapeDtypeStruct((tok_count,...  5.88 us
    unnamed x10, local copies, waits for them, and re-layouts  5.45 us
    all_to_all x1, starting transfers between devices, routed_part(): back = lax.all_to_all(out, 'seq', split_axis=0, concat_axis=0, tiled=True)  4.11 us
  transfers between devices with their start and end apart: 3, of which 1 were waited for; matrix products, arithmetic and copies ran while one was open for 2% of the time, Pallas kernels for 16%

profile of v1, /device:TPU:0, one launch (start us, length us, event | category | flops | bytes accessed | tf_op | source)
XLA Modules:
  0.0 170.9 jit_solution(1039382375477690198)
XLA Ops:
  0.0 2.4 %reshape.40 = bf16[3,2,256,4,128]{4,3,2,1,0:T(4,128)(2,1)S(1)} reshape(bf16[3,512,512]{2,1,0:T(8,128)(2,1)} %param.6) | data formatting | bytes 3145728 | tf_op jit(solution)/shard_map/reshape | solution.py:125
  2.4 0.3 copy.14
  2.7 44.0 %all_to_all.10.r_ref = bf16[8,3,256,128]{3,2,1,0:T(8,128)(2,1)S(1)} all-to-all(bf16[8,3,256,128]{3,2,1,0:T(8,128)(2,1)S(1)} %bitcast.15), channel_id=1, replica_groups=mesh['heads'=4,'seq'=8] {'seq'}, dimensions={0} | all-to-all | bytes 3145728 | tf_op jit(solution)/shard_map/all_to_all | solution.py:127
  46.7 0.0 copy-start
  46.7 0.0 copy-start.2
  46.7 0.1 slice.8
  46.8 0.0 copy-start.3
  46.8 0.1 collective-permute-start.1
  46.9 1.8 %copy-done.2 = bf16[3,512,512]{2,1,0:T(8,128)(2,1)S(1)} copy-done((bf16[3,512,512]{2,1,0:T(8,128)(2,1)S(1)}, bf16[3,512,512]{2,1,0:T(8,128)(2,1)}, u32[]{:S(2)}) %copy-start.2) | copy-done | bytes 1572888
  48.6 0.1 slice.6
  48.7 0.0 copy-done
  48.7 2.3 %collective-permute-start = (bf16[2,512,512]{2,1,0:T(8,128)(2,1)S(1)}, bf16[2,512,512]{2,1,0:T(8,128)(2,1)}, u32[]{:S(2)}, u32[]{:S(2)}) collective-permute-start(bf16[2,512,512]{2,1,0:T(8,128)(2,1)S(1)} %slice.6), channel_id=1, source_target_pairs={{0,1},{1,2},{2,3},{3,4},{4,5},{5,6},{6,7},{8,9},{9,10},{10,11},{11... | collective-permute-start | bytes 3145736 | tf_op jit(solution)/shard_map/ppermute | solution.py:63
  51.1 0.0 copy-done.3
  51.1 18.6 %all-gather.1 = s32[8,4,512]{2,1,0:T(4,128)S(1)} all-gather(s32[1,4,512]{2,1,0:T(4,128)S(1)} %bitcast.21), channel_id=2, replica_groups=mesh['heads'=4,'seq'=8] {'seq'}, dimensions={0}, use_global_device_ids=true | all-gather | bytes 73728 | tf_op jit(solution)/shard_map/all_gather | solution.py:124
  69.8 0.1 rev.6
  70.0 1.3 broadcast_in_dim.8.cq_ref
  71.3 0.6 reshape.43.ck_ref
  71.9 0.1 rev.7
  72.0 0.8 copy.16.qpos_ref
  72.8 0.6 copy.17
  73.4 0.0 collective-permute-done.1.kv_ref
  73.4 21.2 %shard_map.56 = bf16[8,256,128]{2,1,0:T(8,128)(2,1)} custom-call(bf16[8,3,256,128]{3,2,1,0:T(8,128)(2,1)} %copy-done, bf16[8,2,256,128]{3,2,1,0:T(8,128)(2,1)} %collective-permute-done.1.kv_ref, s32[8,256,1]{2,1,0:T(8,128)} %broadcast_in_dim.8.cq_ref, s32[8,1,512]{2,1,0:T(1,128)} %reshape.43.ck_ref, s32[256,1]{1,0:T(8,128)} %copy.16.qpos_ref, s32[1,512]{1,0:T(1,128)} %bitcast.20), custom_call_target="tpu_custom_call" | custom-call | tf_op jit(solution)/shard_map/pallas_call | solution.py:142
  94.6 4.1 %all-to-all-start.1 = ((bf16[8,256,128]{2,1,0:T(8,128)(2,1)}), bf16[8,256,128]{2,1,0:T(8,128)(2,1)S(1)}, u32[]{:S(2)}, u32[]{:S(2)}) async-start(bf16[8,256,128]{2,1,0:T(8,128)(2,1)} %shard_map.56), calls=%async_computation.1 | async-start | bytes 1048576 | tf_op jit(solution)/shard_map/all_to_all | solution.py:149
  98.7 0.0 collective-permute-done.prev_ref
  98.7 5.9 %shard_map.55.local_ref = bf16[512,512]{1,0:T(8,128)(2,1)} custom-call(s32[1]{0:T(128)} %bitcast.first_ref, bf16[3,512,512]{2,1,0:T(8,128)(2,1)} %own_ref.1, bf16[2,512,512]{2,1,0:T(8,128)(2,1)} %collective-permute-done.prev_ref), custom_call_target="tpu_custom_call" | custom-call | flops 805306368 | bytes 6291456 | tf_op jit(solution)/shard_map/pallas_call | solution.py:65
  104.6 9.5 %all-to-all-done.1 = bf16[8,256,128]{2,1,0:T(8,128)(2,1)S(1)} async-done(((bf16[8,256,128]{2,1,0:T(8,128)(2,1)}), bf16[8,256,128]{2,1,0:T(8,128)(2,1)S(1)}, u32[]{:S(2)}, u32[]{:S(2)}) %all-to-all-start.1) | async-done | bytes 524320 | tf_op jit(solution)/shard_map/all_to_all | solution.py:149
  114.1 0.0 copy-start.1
  114.1 0.8 copy-done.1
  114.9 53.7 %shard_map.57 = bf16[512,1024]{1,0:T(8,128)(2,1)} custom-call(bf16[512,512]{1,0:T(8,128)(2,1)} %shard_map.55.local_ref, bf16[4,512,128]{2,1,0:T(8,128)(2,1)} %bitcast.16, bf16[512,4096]{1,0:T(8,128)(2,1)} %wl_ref.1, bf16[512,4096]{1,0:T(8,128)(2,1)} %wr_ref.1), custom_call_target="tpu_custom_call" | custom-call | tf_op jit(solution)/shard_map/pallas_call | solution.py:198
  168.6 2.3 %copy.19 = bf16[512,1024]{1,0:T(8,128)(2,1)} copy(bf16[512,1024]{1,0:T(8,128)(2,1)} %shard_map.57) | data formatting | bytes 2097152
  (7 shorter events, 0.1 us)
Async XLA Ops:
  46.7 2.1 %copy-start = (bf16[8,3,256,128]{3,2,1,0:T(8,128)(2,1)}, bf16[8,3,256,128]{3,2,1,0:T(8,128)(2,1)S(1)}, u32[]{:S(2)}) copy-start(bf16[8,3,256,128]{3,2,1,0:T(8,128)(2,1)S(1)} %all_to_all.10.r_ref) | copy-start | bytes 4718596
  46.7 2.0 %copy-start.2 = (bf16[3,512,512]{2,1,0:T(8,128)(2,1)S(1)}, bf16[3,512,512]{2,1,0:T(8,128)(2,1)}, u32[]{:S(2)}) copy-start(bf16[3,512,512]{2,1,0:T(8,128)(2,1)} %own_ref.1) | copy-start | bytes 4718596
  46.8 4.3 %copy-start.3 = (s32[4,512]{1,0:T(4,128)S(1)}, s32[4,512]{1,0:T(4,128)}, u32[]{:S(2)}) copy-start(s32[4,512]{1,0:T(4,128)} %param.7) | copy-start | bytes 24580
  46.8 26.6 %collective-permute-start.1 = (bf16[8,2,256,128]{3,2,1,0:T(8,128)(2,1)S(1)}, bf16[8,2,256,128]{3,2,1,0:T(8,128)(2,1)}, u32[]{:S(2)}, u32[]{:S(2)}) collective-permute-start(bf16[8,2,256,128]{3,2,1,0:T(8,128)(2,1)S(1)} %slice.8), channel_id=1, source_target_pairs={{0,1},{1,0},{2,3},{3,2},{4,5},{5,4},{6,7},{7,6},{8,9},{9,8},{10,11... | collective-permute-start | bytes 3145736 | tf_op jit(solution)/shard_map/ppermute | solution.py:135
  48.7 50.0 %collective-permute-start = (bf16[2,512,512]{2,1,0:T(8,128)(2,1)S(1)}, bf16[2,512,512]{2,1,0:T(8,128)(2,1)}, u32[]{:S(2)}, u32[]{:S(2)}) collective-permute-start(bf16[2,512,512]{2,1,0:T(8,128)(2,1)S(1)} %slice.6), channel_id=1, source_target_pairs={{0,1},{1,2},{2,3},{3,4},{4,5},{5,6},{6,7},{8,9},{9,10},{10,11},{11... | collective-permute-start | bytes 3145736 | tf_op jit(solution)/shard_map/ppermute | solution.py:63
  94.6 19.5 %all-to-all-start.1 = ((bf16[8,256,128]{2,1,0:T(8,128)(2,1)}), bf16[8,256,128]{2,1,0:T(8,128)(2,1)S(1)}, u32[]{:S(2)}, u32[]{:S(2)}) async-start(bf16[8,256,128]{2,1,0:T(8,128)(2,1)} %shard_map.56), calls=%async_computation.1 | async-start | bytes 1048576 | tf_op jit(solution)/shard_map/all_to_all | solution.py:149
  114.1 0.8 copy-start.1

commit v2 on v1

--- a/solution.py
+++ b/solution.py
@@ -73,81 +73,210 @@
     )(where_at, local_qkv, prev)
 
 
-def cluster_kernel(pair, r_ref, kv_ref, cq_ref, ck_ref, qpos_ref, kpos_ref, out_ref):
-    n, rows, _ = out_ref.shape
-
-    def keys(j, which):
-        if pair:
-            return jnp.concatenate([r_ref[j, 1 + which], kv_ref[j, which]], axis=0)
-        return jnp.concatenate([kv_ref[p, j, which] for p in range(kv_ref.shape[0])], axis=0)
-
-    def one_block(b, _):
-        q = r_ref[b, 0]
-        cq = cq_ref[b]
-
-        def scores(j):
-            return dot_nt(q, keys(j, 0)), cq == ck_ref[j]
-
-        s, same = scores(b)
-        s = jnp.where(same & (kpos_ref[...] <= qpos_ref[...]), s, MASKED)
-        top = jnp.max(s, axis=-1, keepdims=True)
-        p = jnp.exp2((s - top) * SCALE2)
-        total = jnp.sum(p, axis=-1, keepdims=True)
-        acc = dot(p.astype(jnp.bfloat16), keys(b, 1))
-
-        def one_chunk(j, carry):
-            top, total, acc = carry
-            s, same = scores(j)
-            s = jnp.where(same, s, MASKED)
-            new_top = jnp.maximum(top, jnp.max(s, axis=-1, keepdims=True))
-            fade = jnp.exp2((top - new_top) * SCALE2)
-            p = jnp.exp2((s - new_top) * SCALE2)
-            total = fade * total + jnp.sum(p, axis=-1, keepdims=True)
-            acc = fade * acc + dot(p.astype(jnp.bfloat16), keys(j, 1))
-            return new_top, total, acc
-
-        top, total, acc = lax.fori_loop(0, b, one_chunk, (top, total, acc))
-        out_ref[b] = (acc / total).astype(jnp.bfloat16)
+def flipped(me, t, n):
+    out = 0
+    bit = 1
+    while bit < n:
+        out = out + lax.rem(lax.div(me, bit) + lax.div(jnp.int32(t), bit), 2) * bit
+        bit *= 2
+    return out
+
+
+def cluster_kernel(n, heads, qkv_ref, id_ref, out_ref, rq, kv, ck, cq, acc, top, total, done,
+                   own_sem, q_sem, kv_sem, id_sem, pass_sem, back_sem):
+    group = n // heads
+    tok_count = out_ref.shape[1]
+    rows = tok_count // group
+    tile = min(256, tok_count)
+    me = lax.axis_index("seq")
+    head = lax.div(me, group)
+    part = lax.rem(me, group)
+
+    def rows_of(p):
+        return pl.ds(pl.multiple_of(p * rows, rows), rows)
+
+    def remote(src, dst, sem, index, device):
+        return pltpu.make_async_remote_copy(
+            src_ref=src, dst_ref=dst, send_sem=sem.at[(0,) + index], recv_sem=sem.at[(1,) + index],
+            device_id={"seq": device}, device_id_type=MESH)
+
+    def copies(t):
+        d = flipped(me, t, n)
+        h = pl.ds(pl.multiple_of(lax.div(d, group) * DH, DH), DH)
+        p = rows_of(lax.rem(d, group))
+        return (
+            remote(id_ref.at[lax.div(d, group)], ck.at[me], id_sem, (t,), d),
+            remote(qkv_ref.at[pl.ds(1, 2), p, h], kv.at[me, :, p], kv_sem, (t,), d),
+            remote(qkv_ref.at[0, p, h], rq.at[me], q_sem, (t,), d),
+        )
+
+    def passed(u, g):
+        src = kv.at[pl.ds(flipped(head, u, heads) * group, group), :, rows_of(part)]
+        return remote(src, src, pass_sem, (u, g - 1), flipped(me, g, n))
+
+    barrier = pltpu.get_barrier_semaphore()
+
+    def greet(t, _):
+        pl.semaphore_signal(barrier, inc=1, device_id={"seq": flipped(me, t, n)},
+                            device_id_type=MESH)
         return 0
 
-    lax.fori_loop(0, n, one_block, 0)
+    lax.fori_loop(1, n, greet, 0)
+    my_cols = pl.ds(pl.multiple_of(head * DH, DH), DH)
+    own = (
+        pltpu.make_async_copy(id_ref.at[head], ck.at[me], own_sem.at[0]),
+        pltpu.make_async_copy(qkv_ref.at[pl.ds(1, 2), rows_of(part), my_cols],
+                              kv.at[me, :, rows_of(part)], own_sem.at[1]),
+        pltpu.make_async_copy(qkv_ref.at[0, rows_of(part), my_cols], rq.at[me], own_sem.at[2]),
+    )
+    for copy in own:
+        copy.start()
+    pl.semaphore_wait(barrier, n - 1)
+
+    def send(t, _):
+        for copy in copies(t):
+            copy.start()
+        return 0
+
+    lax.fori_loop(1, n, send, 0)
+
+    def update(qg, kg, c, r, diagonal):
+        blocks = min(2, group)
+        if diagonal and group == 2 and rows == tile:
+            blocks = r + 1
+        span = blocks * tok_count
+        at = slice(r * tile, (r + 1) * tile)
+        first = kg * group + c * 2
+        per = tile // rows
+        q = rq[pl.ds(qg * group + r * per, per)].reshape(tile, DH)
+        k = kv[pl.ds(first, blocks), 0].reshape(span, DH)
+        v = kv[pl.ds(first, blocks), 1].reshape(span, DH)
+        ids = jnp.concatenate([ck[first + i] for i in range(blocks)], axis=1)
+        allowed = cq[qg, at, :1] == ids.astype(jnp.float32)
+        if diagonal:
+            i = r * tile + lax.broadcasted_iota(jnp.int32, (tile, 1), 0)
+            shift = rows.bit_length() - 1
+            place = (i >> shift) * tok_count + part * rows + (i & (rows - 1))
+            key = c * 2 * tok_count + lax.broadcasted_iota(jnp.int32, (1, span), 1)
+            allowed = allowed & (key <= place)
+        s = jnp.where(allowed, dot_nt(q, k), MASKED)
+        old = top[qg, at]
+        new = jnp.maximum(old, jnp.max(s, axis=-1, keepdims=True))
+        fade = jnp.exp2((old - new) * SCALE2)
+        p = jnp.exp2((s - new) * SCALE2)
+        top[qg, at] = new
+        total[qg, at] = fade * total[qg, at] + jnp.sum(p, axis=-1, keepdims=True)
+        acc[qg, at] = fade * acc[qg, at] + dot(p.astype(jnp.bfloat16), v)
+
+    def updates(qg, kg, diagonal):
+        def chunk(c, _):
+            for r in range(tok_count // tile):
+                update(qg, kg, c, r, diagonal)
+            return 0
+
+        if group <= 2:
+            chunk(0, 0)
+        else:
+            lax.fori_loop(0, group // 2, chunk, 0)
+
+    def back(t):
+        d = flipped(me, t, n)
+        return remote(done.at[d], out_ref.at[head, rows_of(part)], back_sem, (t,), d)
+
+    own_back = pltpu.make_async_copy(done.at[me], out_ref.at[head, rows_of(part)], own_sem.at[3])
+
+    def finish(v):
+        g = flipped(head, v, heads)
+        o = (acc[g] / total[g]).astype(jnp.bfloat16)
+        done[pl.ds(g * group, group)] = o.reshape(group, rows, DH)
+        if v == 0:
+            own_back.start()
+
+        def give(t, _):
+            back(t).start()
+            return 0
+
+        lax.fori_loop(max(v * group, 1), (v + 1) * group, give, 0)
+
+    for u in range(heads):
+        if u == 0:
+            for copy in own:
+                copy.wait()
+
+        def arrive(t, _):
+            for copy in copies(t):
+                copy.wait_recv()
+            return 0
+
+        lax.fori_loop(max(u * group, 1), (u + 1) * group, arrive, 0)
+        for g in range(1, group):
+            passed(u, g).start()
+        a = flipped(head, u, heads)
+
+        def prepare(w, _):
+            row = ck[a * group + w].astype(jnp.float32)
+            column = jnp.transpose(jnp.broadcast_to(row, (128, tok_count)))
+            done_rows = pl.ds(pl.multiple_of(w * rows, rows), rows)
+            acc[a] = column
+            cq[a, done_rows] = acc[a, rows_of(part)]
+            return 0
+
+        lax.fori_loop(0, group, prepare, 0)
+        top[a] = jnp.full(top.shape[1:], MASKED, jnp.float32)
+        total[a] = jnp.zeros(total.shape[1:], jnp.float32)
+        acc[a] = jnp.zeros(acc.shape[1:], jnp.float32)
+        for g in range(1, group):
+            passed(u, g).wait_recv()
+        updates(a, a, True)
+        for v in reversed(range(u)):
+            b = flipped(head, v, heads)
+            updates(jnp.maximum(a, b), jnp.minimum(a, b), False)
+            if u == heads - 1:
+                finish(v)
+    finish(heads - 1)
+
+    def settle(t, _):
+        for copy in copies(t):
+            copy.wait_send()
+        back(t).wait()
+        return 0
+
+    lax.fori_loop(1, n, settle, 0)
+    own_back.wait()
+    for u in range(heads):
+        for g in range(1, group):
+            passed(u, g).wait_send()
 
 
 def routed_part(routed_qkv, clusters):
     tok_count = routed_qkv.shape[1]
-    head_count = clusters.shape[0]
+    heads = clusters.shape[0]
     n = lax.axis_size("seq")
-    me = lax.axis_index("seq")
-    group = n // head_count
+    group = n // heads
     rows = tok_count // group
-    part = me % group
-    table = lax.all_gather(clusters, "seq")
-    send = routed_qkv.reshape(3, group, rows, head_count, DH).transpose(3, 1, 0, 2, 4)
-    send = send.reshape(n, 3, rows, DH)
-    got = lax.all_to_all(send, "seq", split_axis=0, concat_axis=0, tiled=True)
-    mine = lax.dynamic_index_in_dim(table, me // group, 1, keepdims=False)
-    by_part = mine.reshape(n, group, rows)
-    cq = lax.dynamic_index_in_dim(by_part, part, 1, keepdims=False)[:, :, None]
-    at = jnp.arange(tok_count, dtype=jnp.int32).reshape(group, rows)
-    qpos = lax.dynamic_index_in_dim(at, part, 0, keepdims=False)[:, None]
-    pair = group == 2
-    if pair:
-        other = lax.ppermute(got[:, 1:], "seq", [(i, i + 1 - 2 * (i % 2)) for i in range(n)])
-        ck = jnp.where(part == 0, by_part, by_part[:, ::-1])
-        kpos = jnp.where(part == 0, at, at[::-1])
-    else:
-        groups = [[h * group + p for p in range(group)] for h in range(head_count)]
-        other = lax.all_gather(got[:, 1:], "seq", axis_index_groups=groups)
-        ck, kpos = by_part, at
-    out = pl.pallas_call(
-        functools.partial(cluster_kernel, pair),
-        out_shape=jax.ShapeDtypeStruct((n, rows, DH), jnp.bfloat16),
-        in_specs=[vmem()] * 6,
+    DMA = pltpu.SemaphoreType.DMA
+    return pl.pallas_call(
+        functools.partial(cluster_kernel, n, heads),
+        out_shape=jax.ShapeDtypeStruct((heads, tok_count, DH), jnp.bfloat16),
+        in_specs=[vmem()] * 2,
         out_specs=vmem(),
-        compiler_params=pltpu.CompilerParams(vmem_limit_bytes=VMEM_LIMIT),
-    )(got, other, cq, ck.reshape(n, 1, tok_count), qpos, kpos.reshape(1, tok_count))
-    back = lax.all_to_all(out, "seq", split_axis=0, concat_axis=0, tiled=True)
-    return back.reshape(head_count, tok_count, DH)
+        scratch_shapes=[
+            pltpu.VMEM((n, rows, DH), jnp.bfloat16),
+            pltpu.VMEM((n, 2, tok_count, DH), jnp.bfloat16),
+            pltpu.VMEM((n, 1, tok_count), jnp.int32),
+            pltpu.VMEM((heads, tok_count, 128), jnp.float32),
+            pltpu.VMEM((heads, tok_count, DH), jnp.float32),
+            pltpu.VMEM((heads, tok_count, 1), jnp.float32),
+            pltpu.VMEM((heads, tok_count, 1), jnp.float32),
+            pltpu.VMEM((n, rows, DH), jnp.bfloat16),
+            DMA((4,)), DMA((2, n)), DMA((2, n)), DMA((2, n)),
+            DMA((2, heads, max(group - 1, 1))), DMA((2, n)),
+        ],
+        cost_estimate=pl.CostEstimate(
+            flops=4 << 30, bytes_accessed=200 << 20, transcendentals=8 << 20),
+        compiler_params=pltpu.CompilerParams(
+            vmem_limit_bytes=VMEM_LIMIT, collective_id=1, has_side_effects=True),
+    )(routed_qkv, clusters.reshape(heads, 1, tok_count))
 
 
 def project_kernel(n, local_ref, routed_ref, wl_ref, wr_ref, out_ref,

time: 171 us -> 143 us (0.84)
  the two profiles are of different devices: /device:TPU:0 before, /device:TPU:16 now
where the time goes in v2:
time: 143 us; the launch traced here: 140 us
  Pallas kernels  132 us (92%)
  local copies, waits for them, and re-layouts  5.82 us (4%)
  starting transfers between devices  1.92 us (1%)
    pallas_call x1, Pallas kernels, routed_part(): pl.pallas_call(functools.partial(cluster_kernel, n, heads), out_shape=jax...  72 us
    pallas_call x1, Pallas kernels, project(): pl.pallas_call(functools.partial(project_kernel, n), out_shape=jax.ShapeD...  54.3 us
    pallas_call x1, Pallas kernels, window_part(): pl.pallas_call(window_kernel, out_shape=jax.ShapeDtypeStruct((tok_count,...  5.89 us
    unnamed x3, local copies, waits for them, and re-layouts  3.23 us
  transfers between devices with their start and end apart: 1, of which 0 were waited for; matrix products, arithmetic and copies ran while one was open for 1% of the time, Pallas kernels for 51%

profile of v2, /device:TPU:16, one launch (start us, length us, event | category | flops | bytes accessed | tf_op | source)
XLA Modules:
  0.0 140.0 jit_solution(6120244363956379852)
XLA Ops:
  0.0 1.3 slice.3
  1.3 1.9 %collective-permute-start = (bf16[2,512,512]{2,1,0:T(8,128)(2,1)S(1)}, bf16[2,512,512]{2,1,0:T(8,128)(2,1)S(1)}, u32[]{:S(2)}, u32[]{:S(2)}) collective-permute-start(bf16[2,512,512]{2,1,0:T(8,128)(2,1)S(1)} %slice.3), channel_id=1, source_target_pairs={{0,1},{1,2},{2,3},{3,4},{4,5},{5,6},{6,7},{8,9},{9,10},{10,11},{11... | collective-permute-start | bytes 3145736 | tf_op jit(solution)/shard_map/ppermute | solution.py:63
  3.2 1.3 reshape.7.id_ref
  4.5 72.0 %shard_map.56.routed_ref = bf16[4,512,128]{2,1,0:T(8,128)(2,1)} custom-call(bf16[3,512,512]{2,1,0:T(8,128)(2,1)} %qkv_ref.1, s32[4,1,512]{2,1,0:T(1,128)} %reshape.7.id_ref), custom_call_target="tpu_custom_call" | custom-call | flops 4294967296 | bytes 209715200 | tf_op jit(solution)/shard_map/pallas_call | solution.py:258
  76.6 0.0 collective-permute-done.prev_ref
  76.6 0.0 copy-start
  76.6 1.0 copy-done
  77.5 5.9 %shard_map.55.local_ref = bf16[512,512]{1,0:T(8,128)(2,1)} custom-call(s32[1]{0:T(128)} %bitcast.first_ref, bf16[3,512,512]{2,1,0:T(8,128)(2,1)} %own_ref.1, bf16[2,512,512]{2,1,0:T(8,128)(2,1)} %copy-done), custom_call_target="tpu_custom_call" | custom-call | flops 805306368 | bytes 6291456 | tf_op jit(solution)/shard_map/pallas_call | solution.py:65
  83.4 54.3 %shard_map.57 = bf16[512,1024]{1,0:T(8,128)(2,1)} custom-call(bf16[512,512]{1,0:T(8,128)(2,1)} %shard_map.55.local_ref, bf16[4,512,128]{2,1,0:T(8,128)(2,1)} %shard_map.56.routed_ref, bf16[512,4096]{1,0:T(8,128)(2,1)} %wl_ref.1, bf16[512,4096]{1,0:T(8,128)(2,1)} %wr_ref.1), custom_call_target="tpu_custom_call" | custom-call | tf_op jit(solution)/shard_map/pallas_call | solution.py:327
  137.7 2.3 %copy.7 = bf16[512,1024]{1,0:T(8,128)(2,1)} copy(bf16[512,1024]{1,0:T(8,128)(2,1)} %shard_map.57) | data formatting | bytes 2097152
Async XLA Ops:
  1.3 75.3 %collective-permute-start = (bf16[2,512,512]{2,1,0:T(8,128)(2,1)S(1)}, bf16[2,512,512]{2,1,0:T(8,128)(2,1)S(1)}, u32[]{:S(2)}, u32[]{:S(2)}) collective-permute-start(bf16[2,512,512]{2,1,0:T(8,128)(2,1)S(1)} %slice.3), channel_id=1, source_target_pairs={{0,1},{1,2},{2,3},{3,4},{4,5},{5,6},{6,7},{8,9},{9,10},{10,11},{11... | collective-permute-start | bytes 3145736 | tf_op jit(solution)/shard_map/ppermute | solution.py:63
  76.6 1.0 copy-start

commit v3 on v2

--- a/solution.py
+++ b/solution.py
@@ -30,11 +30,10 @@
     return jnp.dot(a, b, preferred_element_type=jnp.float32)
 
 
-def window_kernel(first_ref, own_ref, prev_ref, out_ref):
+def window_heads(is_first, own_ref, prev_ref, out_ref):
     tok_count, width = out_ref.shape
     rows = min(256, tok_count)
     span = rows + WINDOW
-    is_first = first_ref[0] == 0
     for i in range(tok_count // rows):
         r = lax.broadcasted_iota(jnp.int32, (rows, span), 0)
         c = lax.broadcasted_iota(jnp.int32, (rows, span), 1)
@@ -56,23 +55,6 @@
             out_ref[i * rows:(i + 1) * rows, cols] = o.astype(jnp.bfloat16)
 
 
-def window_part(local_qkv):
-    tok_count = local_qkv.shape[1]
-    width = local_qkv.shape[2]
-    n = lax.axis_size("seq")
-    prev = lax.ppermute(local_qkv[1:], "seq", [(i, i + 1) for i in range(n - 1)])
-    where_at = lax.axis_index("seq").astype(jnp.int32).reshape(1)
-    return pl.pallas_call(
-        window_kernel,
-        out_shape=jax.ShapeDtypeStruct((tok_count, width), jnp.bfloat16),
-        in_specs=[pl.BlockSpec(memory_space=pltpu.SMEM), vmem(), vmem()],
-        out_specs=vmem(),
-        cost_estimate=pl.CostEstimate(
-            flops=4 * tok_count * 768 * width, bytes_accessed=6 << 20, transcendentals=2 << 20),
-        compiler_params=pltpu.CompilerParams(vmem_limit_bytes=VMEM_LIMIT),
-    )(where_at, local_qkv, prev)
-
-
 def flipped(me, t, n):
     out = 0
     bit = 1
@@ -82,8 +64,8 @@
     return out
 
 
-def cluster_kernel(n, heads, qkv_ref, id_ref, out_ref, rq, kv, ck, cq, acc, top, total, done,
-                   own_sem, q_sem, kv_sem, id_sem, pass_sem, back_sem):
+def attention_kernel(n, heads, qkv_ref, id_ref, local_ref, out_ref, local_out_ref, prev, rq, kv, ck, cq, acc, top, total, done,
+                   own_sem, q_sem, kv_sem, id_sem, pass_sem, back_sem, prev_sem):
     group = n // heads
     tok_count = out_ref.shape[1]
     rows = tok_count // group
@@ -139,6 +121,15 @@
         return 0
 
     lax.fori_loop(1, n, send, 0)
+    prev_copy = remote(local_ref.at[pl.ds(1, 2)], prev, prev_sem, (), lax.rem(me + 1, n))
+
+    @pl.when(me < n - 1)
+    def _():
+        prev_copy.start()
+
+    @pl.when(me == 0)
+    def _():
+        prev[...] = jnp.zeros_like(prev)
 
     def update(qg, kg, c, r, diagonal):
         blocks = min(2, group)
@@ -235,6 +226,16 @@
                 finish(v)
     finish(heads - 1)
 
+    @pl.when(me > 0)
+    def _():
+        prev_copy.wait_recv()
+
+    window_heads(me == 0, local_ref, prev, local_out_ref)
+
+    @pl.when(me < n - 1)
+    def _():
+        prev_copy.wait_send()
+
     def settle(t, _):
         for copy in copies(t):
             copy.wait_send()
@@ -248,7 +249,7 @@
             passed(u, g).wait_send()
 
 
-def routed_part(routed_qkv, clusters):
+def attention(local_qkv, routed_qkv, clusters):
     tok_count = routed_qkv.shape[1]
     heads = clusters.shape[0]
     n = lax.axis_size("seq")
@@ -256,11 +257,15 @@
     rows = tok_count // group
     DMA = pltpu.SemaphoreType.DMA
     return pl.pallas_call(
-        functools.partial(cluster_kernel, n, heads),
-        out_shape=jax.ShapeDtypeStruct((heads, tok_count, DH), jnp.bfloat16),
-        in_specs=[vmem()] * 2,
-        out_specs=vmem(),
+        functools.partial(attention_kernel, n, heads),
+        out_shape=(
+            jax.ShapeDtypeStruct((heads, tok_count, DH), jnp.bfloat16),
+            jax.ShapeDtypeStruct(local_qkv.shape[1:], jnp.bfloat16),
+        ),
+        in_specs=[vmem()] * 3,
+        out_specs=(vmem(), vmem()),
         scratch_shapes=[
+            pltpu.VMEM((2,) + local_qkv.shape[1:], jnp.bfloat16),
             pltpu.VMEM((n, rows, DH), jnp.bfloat16),
             pltpu.VMEM((n, 2, tok_count, DH), jnp.bfloat16),
             pltpu.VMEM((n, 1, tok_count), jnp.int32),
@@ -270,62 +275,74 @@
             pltpu.VMEM((heads, tok_count, 1), jnp.float32),
             pltpu.VMEM((n, rows, DH), jnp.bfloat16),
             DMA((4,)), DMA((2, n)), DMA((2, n)), DMA((2, n)),
-            DMA((2, heads, max(group - 1, 1))), DMA((2, n)),
+            DMA((2, heads, max(group - 1, 1))), DMA((2, n)), DMA((2,)),
         ],
         cost_estimate=pl.CostEstimate(
             flops=4 << 30, bytes_accessed=200 << 20, transcendentals=8 << 20),
         compiler_params=pltpu.CompilerParams(
             vmem_limit_bytes=VMEM_LIMIT, collective_id=1, has_side_effects=True),
-    )(routed_qkv, clusters.reshape(heads, 1, tok_count))
-
-
-def project_kernel(n, local_ref, routed_ref, wl_ref, wr_ref, out_ref,
+    )(routed_qkv, clusters.reshape(heads, 1, tok_count), local_qkv)
+
+
+def project_kernel(local_ref, routed_ref, wl_ref, wr_ref, out_ref,
                    x, send, recv, send_sem, recv_sem):
     me = lax.axis_index("heads")
     tok_count, cols = out_ref.shape
+    pieces = send.shape[1]
+    tile = cols // pieces
+    across = (me + 1 - 2 * lax.rem(me, 2), lax.rem(me + 2, 4))
+    corner = lax.rem(across[0] + 2, 4)
     barrier = pltpu.get_barrier_semaphore()
-    for k in range(1, n):
-        pl.semaphore_signal(barrier, inc=1, device_id={"heads": lax.rem(me + k, n)},
-                            device_id_type=MESH)
+    for device in across:
+        pl.semaphore_signal(barrier, inc=1, device_id={"heads": device}, device_id_type=MESH)
     for h in range(routed_ref.shape[0]):
         x[:, h * DH:(h + 1) * DH] = routed_ref[h]
-    tile = min(512, cols)
 
     def product(owner, c):
         at = pl.ds(pl.multiple_of(owner * cols + c * tile, tile), tile)
         return dot(local_ref[...], wl_ref[:, at]) + dot(x[...], wr_ref[:, at])
 
-    copies = []
-    for k in range(1, n):
-        owner = lax.rem(me + k, n)
-        for c in range(cols // tile):
-            send[k - 1, c] = product(owner, c).astype(jnp.bfloat16)
-            if k == 1 and c == 0:
-                pl.semaphore_wait(barrier, n - 1)
-            copy = pltpu.make_async_remote_copy(
-                src_ref=send.at[k - 1, c], dst_ref=recv.at[k - 1, c],
-                send_sem=send_sem.at[k - 1, c], recv_sem=recv_sem.at[k - 1, c],
-                device_id={"heads": owner}, device_id_type=MESH)
-            copy.start()
-            copies.append(copy)
-    for c in range(cols // tile):
-        total = product(me, c).astype(jnp.bfloat16).astype(jnp.float32)
-        for k in range(1, n):
-            copies[(k - 1) * (cols // tile) + c].wait_recv()
-            total = total + recv[k - 1, c].astype(jnp.float32)
-        out_ref[:, c * tile:(c + 1) * tile] = total.astype(jnp.bfloat16)
-    for copy in copies:
+    def hand(kind, c, value, device):
+        send[kind, c] = value.astype(jnp.bfloat16)
+        return pltpu.make_async_remote_copy(
+            src_ref=send.at[kind, c], dst_ref=recv.at[kind, c],
+            send_sem=send_sem.at[kind, c], recv_sem=recv_sem.at[kind, c],
+            device_id={"heads": device}, device_id_type=MESH)
+
+    order = [c + half * (pieces // 2) for c in range(pieces // 2) for half in range(2)]
+    way = [c // (pieces // 2) for c in range(pieces)]
+    copies = {}
+    for kind in range(2):
+        for c in order:
+            device = across[way[c]]
+            copies[kind, c] = hand(kind, c, product(device if kind else corner, c), device)
+            if not kind and c == order[0]:
+                pl.semaphore_wait(barrier, 2)
+            copies[kind, c].start()
+    for c in order:
+        device = across[1 - way[c]]
+        value = product(device, c)
+        copies[0, c].wait_recv()
+        copies[2, c] = hand(2, c, value + recv[0, c].astype(jnp.float32), device)
+        copies[2, c].start()
+    for c in order:
+        value = product(me, c)
+        copies[1, c].wait_recv()
+        value = value + recv[1, c].astype(jnp.float32)
+        copies[2, c].wait_recv()
+        value = value + recv[2, c].astype(jnp.float32)
+        out_ref[:, c * tile:(c + 1) * tile] = value.astype(jnp.bfloat16)
+    for copy in copies.values():
         copy.wait_send()
 
 
 def project(local_out, routed_out, wo_local, wo_routed):
-    n = lax.axis_size("heads")
     tok_count = local_out.shape[0]
-    cols = wo_local.shape[1] // n
-    tile = min(512, cols)
-    slots = (n - 1, cols // tile, tok_count, tile)
+    cols = wo_local.shape[1] // lax.axis_size("heads")
+    pieces = 4
+    slots = (3, pieces, tok_count, cols // pieces)
     return pl.pallas_call(
-        functools.partial(project_kernel, n),
+        project_kernel,
         out_shape=jax.ShapeDtypeStruct((tok_count, cols), jnp.bfloat16),
         in_specs=[vmem()] * 4,
         out_specs=vmem(),
@@ -342,8 +359,7 @@
 
 
 def body(local_qkv, routed_qkv, clusters, wo_local, wo_routed):
-    routed_out = routed_part(routed_qkv, clusters)
-    local_out = window_part(local_qkv)
+    routed_out, local_out = attention(local_qkv, routed_qkv, clusters)
     return project(local_out, routed_out, wo_local, wo_routed)
 
 

time: 143 us -> 111 us (0.78); the launches traced: 140 us -> 111 us
  Pallas kernels: 132 us -> 107 us
  local copies, waits for them, and re-layouts: 5.82 us -> 3.56 us
  starting transfers between devices: 1.92 us -> 0 us
    pallas_call x3 -> x2, Pallas kernels: 132 us -> 107 us  [the longest x1 64.9 us: attention(): pl.pallas_call(functools.partial(attention_kernel, n, heads), out_shape=(...]
    ppermute x1 -> x0, starting transfers between devices: 1.92 us -> none  [window_part(): lax.ppermute(local_qkv[1:], 'seq', [(i, i + 1) for i in range(n - 1)])]
    unnamed x3 -> x1, local copies, waits for them, and re-layouts: 3.23 us -> 2.26 us
  transfers between devices with their start and end apart: 1 -> 0, of which waited for: 0 -> 0; matrix products, arithmetic and copies ran while one was open for 1% -> 0% of each run, Pallas kernels for 51% -> 0%
where the time goes in v3:
time: 111 us
  Pallas kernels  107 us (96%)
  local copies, waits for them, and re-layouts  3.56 us (3%)
    pallas_call x1, Pallas kernels, attention(): pl.pallas_call(functools.partial(attention_kernel, n, heads), out_shape=(...  64.9 us
    pallas_call x1, Pallas kernels, project(): pl.pallas_call(project_kernel, out_shape=jax.ShapeDtypeStruct((tok_count,...  42.4 us
    unnamed x1, local copies, waits for them, and re-layouts  2.26 us

profile of v3, /device:TPU:16, one launch (start us, length us, event | category | flops | bytes accessed | tf_op | source)
XLA Modules:
  0.0 110.8 jit_solution(10566316600137287261)
XLA Ops:
  0.0 1.3 %reshape.3.id_ref = s32[4,1,512]{2,1,0:T(1,128)} reshape(s32[4,512]{1,0:T(4,128)} %param.7) | data formatting | bytes 16384 | tf_op jit(solution)/shard_map/reshape | solution.py:284
  1.3 64.9 %shard_map.55 = (bf16[4,512,128]{2,1,0:T(8,128)(2,1)}, bf16[512,512]{1,0:T(8,128)(2,1)}) custom-call(bf16[3,512,512]{2,1,0:T(8,128)(2,1)} %qkv_ref.1, s32[4,1,512]{2,1,0:T(1,128)} %reshape.3.id_ref, bf16[3,512,512]{2,1,0:T(8,128)(2,1)} %local_ref.1), custom_call_target="tpu_custom_call" | custom-call | flops 4294967296 | bytes 209715200 | tf_op jit(solution)/shard_map/pallas_call | solution.py:259
  66.2 42.4 %shard_map.56 = bf16[512,1024]{1,0:T(8,128)(2,1)} custom-call(bf16[512,512]{1,0:T(8,128)(2,1)} %get-tuple-element.7.local_ref, bf16[4,512,128]{2,1,0:T(8,128)(2,1)} %get-tuple-element.8.routed_ref, bf16[512,4096]{1,0:T(8,128)(2,1)} %wl_ref.1, bf16[512,4096]{1,0:T(8,128)(2,1)} %wr_ref.1), custom_call_target="tpu_custom_call" | custom-call | tf_op jit(solution)/shard_map/pallas_call | solution.py:344
  108.6 2.3 %copy.7 = bf16[512,1024]{1,0:T(8,128)(2,1)} copy(bf16[512,1024]{1,0:T(8,128)(2,1)} %shard_map.56) | data formatting | bytes 2097152

commit v4 on v3

--- a/solution.py
+++ b/solution.py
@@ -64,10 +64,11 @@
     return out
 
 
-def attention_kernel(n, heads, qkv_ref, id_ref, local_ref, out_ref, local_out_ref, prev, rq, kv, ck, cq, acc, top, total, done,
-                   own_sem, q_sem, kv_sem, id_sem, pass_sem, back_sem, prev_sem):
+def layer_kernel(n, heads, qkv_ref, id_ref, local_ref, wl_any, wr_any, out_ref, prev, rq, kv, ck, cq, acc, top, total, done,
+                   own_sem, q_sem, kv_sem, id_sem, pass_sem, back_sem, prev_sem,
+                 local_out, x, wl, wr, tiles_out, tiles_in, out_sem, in_sem, w_sem):
     group = n // heads
-    tok_count = out_ref.shape[1]
+    tok_count = x.shape[0]
     rows = tok_count // group
     tile = min(256, tok_count)
     me = lax.axis_index("seq")
@@ -104,6 +105,14 @@
         return 0
 
     lax.fori_loop(1, n, greet, 0)
+    place = lax.axis_index("heads")
+    across = (place + 1 - 2 * lax.rem(place, 2), lax.rem(place + 2, 4))
+    for device in across:
+        pl.semaphore_signal(barrier, inc=1, device_id={"heads": device}, device_id_type=MESH)
+    weights = (
+        pltpu.make_async_copy(wl_any, wl, w_sem.at[0]),
+        pltpu.make_async_copy(wr_any, wr, w_sem.at[1]),
+    )
     my_cols = pl.ds(pl.multiple_of(head * DH, DH), DH)
     own = (
         pltpu.make_async_copy(id_ref.at[head], ck.at[me], own_sem.at[0]),
@@ -113,7 +122,7 @@
     )
     for copy in own:
         copy.start()
-    pl.semaphore_wait(barrier, n - 1)
+    pl.semaphore_wait(barrier, n - 1 + len(across))
 
     def send(t, _):
         for copy in copies(t):
@@ -121,6 +130,8 @@
         return 0
 
     lax.fori_loop(1, n, send, 0)
+    for copy in weights:
+        copy.start()
     prev_copy = remote(local_ref.at[pl.ds(1, 2)], prev, prev_sem, (), lax.rem(me + 1, n))
 
     @pl.when(me < n - 1)
@@ -172,9 +183,9 @@
 
     def back(t):
         d = flipped(me, t, n)
-        return remote(done.at[d], out_ref.at[head, rows_of(part)], back_sem, (t,), d)
-
-    own_back = pltpu.make_async_copy(done.at[me], out_ref.at[head, rows_of(part)], own_sem.at[3])
+        return remote(done.at[d], x.at[rows_of(part), my_cols], back_sem, (t,), d)
+
+    own_back = pltpu.make_async_copy(done.at[me], x.at[rows_of(part), my_cols], own_sem.at[3])
 
     def finish(v):
         g = flipped(head, v, heads)
@@ -230,7 +241,7 @@
     def _():
         prev_copy.wait_recv()
 
-    window_heads(me == 0, local_ref, prev, local_out_ref)
+    window_heads(me == 0, local_ref, prev, local_out)
 
     @pl.when(me < n - 1)
     def _():
@@ -247,56 +258,16 @@
     for u in range(heads):
         for g in range(1, group):
             passed(u, g).wait_send()
-
-
-def attention(local_qkv, routed_qkv, clusters):
-    tok_count = routed_qkv.shape[1]
-    heads = clusters.shape[0]
-    n = lax.axis_size("seq")
-    group = n // heads
-    rows = tok_count // group
-    DMA = pltpu.SemaphoreType.DMA
-    return pl.pallas_call(
-        functools.partial(attention_kernel, n, heads),
-        out_shape=(
-            jax.ShapeDtypeStruct((heads, tok_count, DH), jnp.bfloat16),
-            jax.ShapeDtypeStruct(local_qkv.shape[1:], jnp.bfloat16),
-        ),
-        in_specs=[vmem()] * 3,
-        out_specs=(vmem(), vmem()),
-        scratch_shapes=[
-            pltpu.VMEM((2,) + local_qkv.shape[1:], jnp.bfloat16),
-            pltpu.VMEM((n, rows, DH), jnp.bfloat16),
-            pltpu.VMEM((n, 2, tok_count, DH), jnp.bfloat16),
-            pltpu.VMEM((n, 1, tok_count), jnp.int32),
-            pltpu.VMEM((heads, tok_count, 128), jnp.float32),
-            pltpu.VMEM((heads, tok_count, DH), jnp.float32),
-            pltpu.VMEM((heads, tok_count, 1), jnp.float32),
-            pltpu.VMEM((heads, tok_count, 1), jnp.float32),
-            pltpu.VMEM((n, rows, DH), jnp.bfloat16),
-            DMA((4,)), DMA((2, n)), DMA((2, n)), DMA((2, n)),
-            DMA((2, heads, max(group - 1, 1))), DMA((2, n)), DMA((2,)),
-        ],
-        cost_estimate=pl.CostEstimate(
-            flops=4 << 30, bytes_accessed=200 << 20, transcendentals=8 << 20),
-        compiler_params=pltpu.CompilerParams(
-            vmem_limit_bytes=VMEM_LIMIT, collective_id=1, has_side_effects=True),
-    )(routed_qkv, clusters.reshape(heads, 1, tok_count), local_qkv)
-
-
-def project_kernel(local_ref, routed_ref, wl_ref, wr_ref, out_ref,
-                   x, send, recv, send_sem, recv_sem):
-    me = lax.axis_index("heads")
-    tok_count, cols = out_ref.shape
+    for copy in weights:
+        copy.wait()
+    project(place, across, local_out, x, wl, wr, out_ref, tiles_out, tiles_in, out_sem, in_sem)
+
+
+def project(me, across, local_ref, x, wl_ref, wr_ref, out_ref, send, recv, send_sem, recv_sem):
+    cols = out_ref.shape[1]
     pieces = send.shape[1]
     tile = cols // pieces
-    across = (me + 1 - 2 * lax.rem(me, 2), lax.rem(me + 2, 4))
     corner = lax.rem(across[0] + 2, 4)
-    barrier = pltpu.get_barrier_semaphore()
-    for device in across:
-        pl.semaphore_signal(barrier, inc=1, device_id={"heads": device}, device_id_type=MESH)
-    for h in range(routed_ref.shape[0]):
-        x[:, h * DH:(h + 1) * DH] = routed_ref[h]
 
     def product(owner, c):
         at = pl.ds(pl.multiple_of(owner * cols + c * tile, tile), tile)
@@ -316,8 +287,6 @@
         for c in order:
             device = across[way[c]]
             copies[kind, c] = hand(kind, c, product(device if kind else corner, c), device)
-            if not kind and c == order[0]:
-                pl.semaphore_wait(barrier, 2)
             copies[kind, c].start()
     for c in order:
         device = across[1 - way[c]]
@@ -336,31 +305,45 @@
         copy.wait_send()
 
 
-def project(local_out, routed_out, wo_local, wo_routed):
-    tok_count = local_out.shape[0]
+def body(local_qkv, routed_qkv, clusters, wo_local, wo_routed):
+    tok_count = routed_qkv.shape[1]
+    heads = clusters.shape[0]
+    n = lax.axis_size("seq")
+    group = n // heads
+    rows = tok_count // group
     cols = wo_local.shape[1] // lax.axis_size("heads")
-    pieces = 4
-    slots = (3, pieces, tok_count, cols // pieces)
+    slots = (3, 4, tok_count, cols // 4)
+    DMA = pltpu.SemaphoreType.DMA
     return pl.pallas_call(
-        project_kernel,
+        functools.partial(layer_kernel, n, heads),
         out_shape=jax.ShapeDtypeStruct((tok_count, cols), jnp.bfloat16),
-        in_specs=[vmem()] * 4,
+        in_specs=[vmem()] * 3 + [pl.BlockSpec(memory_space=pl.ANY)] * 2,
         out_specs=vmem(),
         scratch_shapes=[
-            pltpu.VMEM((tok_count, wo_routed.shape[0]), jnp.bfloat16),
+            pltpu.VMEM((2,) + local_qkv.shape[1:], jnp.bfloat16),
+            pltpu.VMEM((n, rows, DH), jnp.bfloat16),
+            pltpu.VMEM((n, 2, tok_count, DH), jnp.bfloat16),
+            pltpu.VMEM((n, 1, tok_count), jnp.int32),
+            pltpu.VMEM((heads, tok_count, 128), jnp.float32),
+            pltpu.VMEM((heads, tok_count, DH), jnp.float32),
+            pltpu.VMEM((heads, tok_count, 1), jnp.float32),
+            pltpu.VMEM((heads, tok_count, 1), jnp.float32),
+            pltpu.VMEM((n, rows, DH), jnp.bfloat16),
+            DMA((4,)), DMA((2, n)), DMA((2, n)), DMA((2, n)),
+            DMA((2, heads, max(group - 1, 1))), DMA((2, n)), DMA((2,)),
+            pltpu.VMEM(local_qkv.shape[1:], jnp.bfloat16),
+            pltpu.VMEM((tok_count, heads * DH), jnp.bfloat16),
+            pltpu.VMEM(wo_local.shape, jnp.bfloat16),
+            pltpu.VMEM(wo_routed.shape, jnp.bfloat16),
             pltpu.VMEM(slots, jnp.bfloat16),
             pltpu.VMEM(slots, jnp.bfloat16),
-            pltpu.SemaphoreType.DMA(slots[:2]),
-            pltpu.SemaphoreType.DMA(slots[:2]),
+            DMA(slots[:2]), DMA(slots[:2]), DMA((2,)),
         ],
+        cost_estimate=pl.CostEstimate(
+            flops=4 << 30, bytes_accessed=200 << 20, transcendentals=8 << 20),
         compiler_params=pltpu.CompilerParams(
             vmem_limit_bytes=VMEM_LIMIT, collective_id=0, has_side_effects=True),
-    )(local_out, routed_out, wo_local, wo_routed)
-
-
-def body(local_qkv, routed_qkv, clusters, wo_local, wo_routed):
-    routed_out, local_out = attention(local_qkv, routed_qkv, clusters)
-    return project(local_out, routed_out, wo_local, wo_routed)
+    )(routed_qkv, clusters.reshape(heads, 1, tok_count), local_qkv, wo_local, wo_routed)
 
 
 def solution(mesh):

time: 111 us -> 106 us (0.955)
  Pallas kernels: 107 us -> 102 us
    pallas_call x2 -> x1, Pallas kernels: 107 us -> 102 us  [body(): pl.pallas_call(functools.partial(layer_kernel, n, heads), out_shape=jax.S...]
where the time goes in v4:
time: 106 us
  Pallas kernels  102 us (96%)
  local copies, waits for them, and re-layouts  3.56 us (3%)
    pallas_call x1, Pallas kernels, body(): pl.pallas_call(functools.partial(layer_kernel, n, heads), out_shape=jax.S...  102 us
    unnamed x1, local copies, waits for them, and re-layouts  2.26 us

profile of v4, /device:TPU:16, one launch (start us, length us, event | category | flops | bytes accessed | tf_op | source)
XLA Modules:
  0.0 105.5 jit_solution(8990643937868382413)
XLA Ops:
  0.0 1.3 %reshape.3.id_ref = s32[4,1,512]{2,1,0:T(1,128)} reshape(s32[4,512]{1,0:T(4,128)} %param.7) | data formatting | bytes 16384 | tf_op jit(solution)/shard_map/reshape | solution.py:346
  1.3 102.0 %shard_map.55 = bf16[512,1024]{1,0:T(8,128)(2,1)} custom-call(bf16[3,512,512]{2,1,0:T(8,128)(2,1)} %qkv_ref.1, s32[4,1,512]{2,1,0:T(1,128)} %reshape.3.id_ref, bf16[3,512,512]{2,1,0:T(8,128)(2,1)} %local_ref.1, bf16[512,4096]{1,0:T(8,128)(2,1)} %wl_any.1, bf16[512,4096]{1,0:T(8,128)(2,1)} %wr_any.1), custom_call_target="tpu_custom_call" | custom-call | flops 4294967296 | bytes 209715200 | tf_op jit(solution)/shard_map/pallas_call | solution.py:317
  103.3 2.3 %copy.7 = bf16[512,1024]{1,0:T(8,128)(2,1)} copy(bf16[512,1024]{1,0:T(8,128)(2,1)} %shard_map.55) | data formatting | bytes 2097152
